TPU v7x, 32 devices: a whole 2x2x4 slice. The times are simulated.
32 devices in a mesh: grp: 4 (over y, core), seq: 8 (over z, x).
Axes of the slice: x: 2, y: 2, z: 4, core: 2. Of those that a mesh axis runs over, the one named last changes fastest.
Arguments:
- queries: bfloat16 [16384, 512], P(('grp', 'seq')), may hold values from -8 to 8
- keys: bfloat16 [16384, 512], P(('grp', 'seq')), may hold values from -4.5 to 4.5
- values: bfloat16 [16384, 512], P(('grp', 'seq')), may hold values from -6 to 6
- resid: bfloat16 [16384, 1024], P(('grp', 'seq')), may hold values from -54 to 54
- w_out: bfloat16 [512, 1024], replicated, may hold values from -2 to 2
- block_lang: int32 [256], P(('grp', 'seq')), may hold values from 0 to 11, as said below
- w_down: bfloat16 [12, 1024, 384], P('grp', 'seq'), may hold values from -0.1875 to 0.1875
- w_up: bfloat16 [12, 384, 1024], P('grp', None, 'seq'), may hold values from -0.3125 to 0.3125
- bias_down: bfloat16 [12, 384], P('grp'), may hold values from -4 to 4
- cotangent: bfloat16 [16384, 1024], P(('grp', 'seq')), may hold values from -6 to 6
Outputs:
- grad_down: float32 [1024, 12, 384], P('seq', 'grp')
Inputs may be any that keep to these rules, and one draw needn't show every extreme that they name: Block b holds tokens b * 64 to (b + 1) * 64 - 1, and its language's owner group is block_lang[b] // 3. Of the 8 blocks of one device (blocks d * 8 to (d + 1) * 8 - 1), at most 2 have the same owner group; for every index along seq, some owner group has a block from the device of that index in every group.
All inputs are finite; a program needn't handle non-finite values.
Results may differ from a plain program's by a relative error of at most 0.022.
Values may be sent and summed in bfloat16 or wider, within the bound.
No kernel may reach another device: no remote copies, remote signals or barrier semaphores. Data moves between devices by JAX's collectives and lax.ppermute only.
A program may use at most 128 MiB of HBM per device.

v0:
```python
import math
import jax
import jax.numpy as jnp
from jax import lax
from jax.sharding import PartitionSpec as P

HD = 64
WINDOW = 256
EPSILON = 1e-05


def shifted(value, axis, by):
    size = lax.axis_size(axis)
    pairs = [(i, i + by) for i in range(size) if 0 <= i + by < size]
    return lax.ppermute(value, axis, pairs)


def gelu_slope(pre_act):
    return jax.vjp(jax.nn.gelu, pre_act)[1](jnp.ones_like(pre_act))[0]


def normalize(block_rows):
    widened = block_rows.astype(jnp.float32)
    center = widened - jnp.mean(widened, axis=-1, keepdims=True)
    spread = jnp.mean(center * center, axis=-1, keepdims=True)
    return (center * lax.rsqrt(spread + EPSILON)).astype(jnp.bfloat16)


def body(queries, keys, values, resid, w_out, block_lang, w_down, w_up, bias_down, cotangent):
    tok_dev, width_q = queries.shape
    head_dim = HD
    head_count = width_q // head_dim
    window_len = WINDOW
    k_rim, v_rim = shifted((keys[tok_dev - window_len :], values[tok_dev - window_len :]), "seq", 1)
    key_span = window_len + tok_dev
    q_heads = queries.reshape(tok_dev, head_count, head_dim)
    k_heads = jnp.concatenate([k_rim, keys], axis=0).reshape(key_span, head_count, head_dim)
    v_heads = jnp.concatenate([v_rim, values], axis=0).reshape(key_span, head_count, head_dim)
    scores = jnp.einsum(
        "qhd,khd->hqk", q_heads, k_heads, preferred_element_type=jnp.float32
    ) * head_dim ** (-0.5)
    q_pos = jnp.arange(tok_dev)[:, None] + window_len
    k_pos = jnp.arange(key_span)[None, :]
    first_dev = lax.axis_index("seq") == 0
    allowed = (
        (k_pos <= q_pos)
        & (k_pos > q_pos - window_len)
        & ((k_pos >= window_len) | jnp.logical_not(first_dev))
    )
    scores = jnp.where(allowed[None], scores, -1e30)
    row_max = jnp.max(scores, axis=-1, keepdims=True)
    weights = jnp.exp(scores - row_max) * allowed[None]
    softmax_w = (weights / jnp.sum(weights, axis=-1, keepdims=True)).astype(jnp.bfloat16)
    context = jnp.einsum("hqk,khd->qhd", softmax_w, v_heads, preferred_element_type=jnp.float32)
    context = context.astype(jnp.bfloat16).reshape(tok_dev, width_q)
    hidden = (
        resid.astype(jnp.float32) + jnp.dot(context, w_out, preferred_element_type=jnp.float32)
    ).astype(jnp.bfloat16)
    block_count = block_lang.shape[0]
    block_len = tok_dev // block_count
    group_count = lax.axis_size("grp")
    cap_each = max(1, block_count // group_count)
    slot_count = group_count * cap_each
    lang_grp = w_down.shape[0]
    model_width = hidden.shape[1]
    hidden_units = w_down.shape[2]
    owner_group = block_lang // lang_grp
    block_ids = jnp.arange(block_count)
    earlier = (owner_group[None, :] == owner_group[:, None]) & (
        block_ids[None, :] < block_ids[:, None]
    )
    rank_within = jnp.sum(earlier.astype(jnp.int32), axis=1)
    slot_of = owner_group * cap_each + rank_within
    select_int = (slot_of[None, :] == jnp.arange(slot_count)[:, None]).astype(jnp.int32)
    choose_mat = select_int.astype(jnp.bfloat16)
    outgoing = normalize(hidden)

    def to_slots(token_rows):
        shaped = token_rows.reshape(block_count, block_len, model_width)
        return jnp.einsum(
            "ob,btd->otd", choose_mat, shaped, preferred_element_type=jnp.float32
        ).astype(jnp.bfloat16)

    row_slots = to_slots(outgoing)
    cot_slots = to_slots(cotangent)
    lang_slots = jnp.sum(select_int * block_lang[None, :], axis=1) + jnp.sum(select_int, axis=1) - 1
    got_rows, got_cot, got_lang = (
        lax.all_to_all(row_slots, "grp", split_axis=0, concat_axis=0, tiled=True),
        lax.all_to_all(cot_slots, "grp", split_axis=0, concat_axis=0, tiled=True),
        lax.all_to_all(lang_slots, "grp", split_axis=0, concat_axis=0, tiled=True),
    )
    down_all, up_all = (
        lax.all_gather(w_down, "seq", axis=1, tiled=True),
        lax.all_gather(w_up, "seq", axis=2, tiled=True),
    )
    live_slot = got_lang >= 0
    safe_lang = jnp.where(live_slot, got_lang - lax.axis_index("grp") * lang_grp, 0).astype(
        jnp.int32
    )

    def slot_terms(slot_item):
        slot_rows, slot_cot, language, is_live = slot_item
        down_one = lax.dynamic_index_in_dim(down_all, language, 0, keepdims=False)
        up_one = lax.dynamic_index_in_dim(up_all, language, 0, keepdims=False)
        bias_one = lax.dynamic_index_in_dim(bias_down, language, 0, keepdims=False).astype(
            jnp.float32
        )
        pre_act = jnp.dot(slot_rows, down_one, preferred_element_type=jnp.float32) + bias_one
        back_proj = lax.dot_general(
            slot_cot, up_one, (((1,), (1,)), ((), ())), preferred_element_type=jnp.float32
        )
        gate_grad = (gelu_slope(pre_act) * back_proj * is_live.astype(jnp.float32)).astype(
            jnp.bfloat16
        )
        return (slot_rows, gate_grad)

    normed_all, grad_all = lax.map(slot_terms, (got_rows, got_cot, safe_lang, live_slot))
    inv_scale = 1.0 / math.sqrt(tok_dev * lax.axis_size("seq"))

    def add_slot(slot_idx, running):
        columns = normed_all[slot_idx]
        product = lax.dot_general(
            columns,
            grad_all[slot_idx],
            (((0,), (0,)), ((), ())),
            preferred_element_type=jnp.float32,
        )
        language = safe_lang[slot_idx]
        current = lax.dynamic_index_in_dim(running, language, 1, keepdims=True)
        return lax.dynamic_update_index_in_dim(running, current + product[:, None, :], language, 1)

    start_acc = jnp.zeros(
        (model_width // lax.axis_size("seq") * lax.axis_size("seq"), lang_grp, hidden_units),
        jnp.float32,
    )
    return lax.psum_scatter(
        (lax.fori_loop(0, slot_count, add_slot, start_acc) * inv_scale).astype(jnp.bfloat16),
        "seq",
        scatter_dimension=0,
        tiled=True,
    ).astype(jnp.float32)


def solution(mesh):
    in_specs = (
        P(("grp", "seq"), None),
        P(("grp", "seq"), None),
        P(("grp", "seq"), None),
        P(("grp", "seq"), None),
        P(),
        P(("grp", "seq")),
        P("grp", "seq", None),
        P("grp", None, "seq"),
        P("grp", None),
        P(("grp", "seq"), None),
    )
    out_specs = P("seq", "grp", None)
    return jax.shard_map(body, mesh=mesh, in_specs=in_specs, out_specs=out_specs, check_vma=False)
```

profile of v0, /device:TPU:0, one launch (start us, length us, event | category | flops | bytes accessed | tf_op | source)
XLA Modules:
  0.0 305.9 jit_solution(14016514012558106310)
XLA Ops:
  6.5 0.7 all-gather.3.cloned.1.call-update
  7.3 1.0 slice.7
  8.2 5.6 %collective-permute-start.1 = (bf16[256,512]{1,0:T(8,128)(2,1)S(1)}, bf16[256,512]{1,0:T(8,128)(2,1)}, u32[]{:S(2)}, u32[]{:S(2)}) collective-permute-start(bf16[256,512]{1,0:T(8,128)(2,1)S(1)} %slice.7), channel_id=1, source_target_pairs={{0,1},{1,2},{2,3},{3,4},{4,5},{5,6},{6,7},{8,9},{9,10},{10,11},{11... | collective-permute-start | bytes 786440 | tf_op jit(solution)/shard_map/ppermute | solution.py:15
  13.8 1.7 slice.6
  15.5 3.5 %collective-permute-start = (bf16[256,512]{1,0:T(8,128)(2,1)}, bf16[256,512]{1,0:T(8,128)(2,1)}, u32[]{:S(2)}, u32[]{:S(2)}) collective-permute-start(bf16[256,512]{1,0:T(8,128)(2,1)} %slice.6), channel_id=1, source_target_pairs={{0,1},{1,2},{2,3},{3,4},{4,5},{5,6},{6,7},{8,9},{9,10},{10,11},{11... | collective-permute-start | bytes 786440 | tf_op jit(solution)/shard_map/ppermute | solution.py:15
  20.5 0.8 convert_reduce_fusion.2
  22.0 3.2 %all-to-all-start = ((s32[4,2,1]{1,2,0:T(1,128)}), s32[4,2,1]{1,2,0:T(1,128)S(1)}, u32[]{:S(2)}, u32[]{:S(2)}) async-start(s32[4,2,1]{1,2,0:T(1,128)} %bitcast.11), calls=%async_computation | async-start | bytes 4096 | tf_op jit(solution)/shard_map/all_to_all | solution.py:90
  25.2 0.7 all-gather.5.cloned.1.call-update
  25.9 2.1 copy.50
  28.0 0.7 convolution_convert_fusion
  28.7 1.6 copy.55
  30.3 1.1 fusion.39
  31.4 1.0 pad_maximum_fusion.1
  32.4 1.2 copy.49
  33.6 11.0 %fusion.53 = (f32[8,512]{1,0:T(8,128)S(1)}, f32[8,512,768]{1,2,0:T(8,128)}) fusion(f32[512,768]{0,1:T(8,128)S(1)} %get-tuple-element.273, bf16[768,8,64]{0,2,1:T(8,128)(2,1)} %bitcast.84, bf16[512,8,64]{0,2,1:T(8,128)(2,1)} %bitcast.86, pred[512,768]{0,1:T(8,128)(4,1)} %get-tuple-element.272), kind=kOutput, calls=%fused_computation.85 | convolution fusion | flops 418382592 | bytes 15876096 | tf_op jit(solution)/shard_map/sub | solution.py:52
  44.6 1.0 pad_maximum_fusion
  45.9 6.0 %fusion.40 = bf16[8,64,512]{2,1,0:T(8,128)(2,1)S(1)} fusion(bf16[768,8,64]{0,2,1:T(8,128)(2,1)S(1)} %bitcast.85, f32[8,512,768]{1,2,0:T(8,128)} %get-tuple-element.275, f32[8,512]{1,0:T(8,128)S(1)} %get-tuple-element.274), kind=kOutput, calls=%fused_computation.56 | convolution fusion | flops 409206784 | bytes 13910016 | tf_op jit(solution)/shard_map/hqk,khd->qhd/dot_general | solution.py:54
  51.9 0.8 convert_reduce_fusion.1
  52.8 3.7 %all-to-all-start.2 = ((bf16[8,64,1024]{2,1,0:T(8,128)(2,1)}), bf16[8,64,1024]{2,1,0:T(8,128)(2,1)S(1)}, u32[]{:S(2)}, u32[]{:S(2)}) async-start(bf16[8,64,1024]{2,1,0:T(8,128)(2,1)} %copy.55), calls=%async_computation.2 | async-start | bytes 2097152 | tf_op jit(solution)/shard_map/all_to_all | solution.py:89
  57.2 0.7 convolution_convert_fusion.1
  58.0 1.6 copy.53
  59.5 11.3 %all-to-all-done.2 = bf16[8,64,1024]{2,1,0:T(8,128)(2,1)S(1)} async-done(((bf16[8,64,1024]{2,1,0:T(8,128)(2,1)}), bf16[8,64,1024]{2,1,0:T(8,128)(2,1)S(1)}, u32[]{:S(2)}, u32[]{:S(2)}) %all-to-all-start.2) | async-done | bytes 1048608 | tf_op jit(solution)/shard_map/all_to_all | solution.py:89
  70.8 3.5 %all-to-all-start.1 = ((bf16[8,64,1024]{2,1,0:T(8,128)(2,1)}), bf16[8,64,1024]{2,1,0:T(8,128)(2,1)S(1)}, u32[]{:S(2)}, u32[]{:S(2)}) async-start(bf16[8,64,1024]{2,1,0:T(8,128)(2,1)} %copy.53), calls=%async_computation.1 | async-start | bytes 2097152 | tf_op jit(solution)/shard_map/all_to_all | solution.py:88
  74.5 0.7 ge.18
  75.9 12.8 %all-to-all-done.1 = bf16[8,64,1024]{2,1,0:T(8,128)(2,1)S(1)} async-done(((bf16[8,64,1024]{2,1,0:T(8,128)(2,1)}), bf16[8,64,1024]{2,1,0:T(8,128)(2,1)S(1)}, u32[]{:S(2)}, u32[]{:S(2)}) %all-to-all-start.1) | async-done | bytes 1048608 | tf_op jit(solution)/shard_map/all_to_all | solution.py:88
  88.7 31.4 %all-gather.5.cloned.1.call-done = bf16[3,384,1024]{2,1,0:T(8,128)(2,1)} async-done(((bf16[3,384,128]{2,1,0:T(8,128)(2,1)}), bf16[3,384,1024]{2,1,0:T(8,128)(2,1)}) %all-gather.5.cloned.1.call-update) | async-done | bytes 2359312 | tf_op jit(solution)/shard_map/all_gather | solution.py:94
  120.1 61.8 %while.25 = (s32[]{:T(128)}, bf16[8,64,384]{2,1,0:T(8,128)(2,1)S(1)}, bf16[8,64,1024]{2,1,0:T(8,128)(2,1)S(1)}, s32[8]{0:T(128)S(1)}, bf16[3,1024,384]{2,1,0:T(8...) while((s32[]{:T(128)}, ...), condition=%wide.region_8.9_spmd, body=%wide.region_7.8_spmd.sunk | while | flops 101179776 | bytes 2087354 | solution.py:117
  122.9 1.4 convolution_add_fusion.2
  124.2 1.3 dynamic_slice.120
  126.3 1.5 fusion.73
  130.6 1.4 convolution_add_fusion.2
  132.0 1.3 dynamic_slice.120
  134.0 1.5 fusion.73
  138.3 1.4 convolution_add_fusion.2
  139.7 1.3 dynamic_slice.120
  141.7 1.5 fusion.73
  146.0 1.4 convolution_add_fusion.2
  147.4 1.3 dynamic_slice.120
  149.5 1.5 fusion.73
  153.8 1.4 convolution_add_fusion.2
  155.2 1.3 dynamic_slice.120
  157.2 1.5 fusion.73
  161.5 1.4 convolution_add_fusion.2
  162.9 1.3 dynamic_slice.120
  164.9 1.5 fusion.73
  169.2 1.4 convolution_add_fusion.2
  170.6 1.3 dynamic_slice.120
  172.6 1.5 fusion.73
  176.9 1.4 convolution_add_fusion.2
  178.3 1.3 dynamic_slice.120
  180.4 1.5 fusion.73
  181.9 2.4 broadcast_in_dim.50
  184.3 41.2 %while.26 = (s32[]{:T(128)}, f32[1024,3,384]{2,0,1:T(8,128)}, s32[8]{0:T(128)S(1)}, bf16[8,64,1024]{2,1,0:T(8,128)(2,1)S(1)}, bf16[8,64,384]{2,1,0:T(8,128)(2,1)S(1)}, /*index=5*/s32[]{:T(128)}, s32[]{:T(128)}, s32[]{:T(128)}) while((s32[]{:T(128)}, f32[1024,3,384]{2,0,1:T(8,128)}, s32[8]{0:T(128)S(1)}, bf16[8,64,1024]{2,1,0:T(8,128)(2,1)S(1)}, ...), condition=%wide.region_10.11_spmd, body=%wide.region_9.10_spmd.sunk | while | flops 50724868 | bytes 3327111 | solution.py:137
  186.5 3.0 fusion.76
  191.7 3.0 fusion.76
  196.8 2.9 fusion.76
  202.0 2.9 fusion.76
  207.1 2.9 fusion.76
  212.3 2.9 fusion.76
  217.4 3.0 fusion.76
  222.6 2.9 fusion.76
  225.5 4.2 %multiply_convert_fusion = bf16[1024,3,384]{2,0,1:T(8,128)(2,1)} fusion(f32[1024,3,384]{2,0,1:T(8,128)} %get-tuple-element.213), kind=kLoop, calls=%fused_computation.42 | loop fusion | flops 2359296 | bytes 7077888 | tf_op jit(solution)/shard_map/convert_element_type | solution.py:137
  229.7 67.9 %reduce-scatter.2.cloned.1.call-done = bf16[128,3,384]{2,0,1:T(8,128)(2,1)} async-done(((bf16[1024,3,384]{2,0,1:T(8,128)(2,1)}), bf16[128,3,384]{2,0,1:T(8,128)(2,1)}) %reduce-scatter.2.cloned.1.call-update) | async-done | bytes 294928 | tf_op jit(solution)/shard_map/reduce_scatter | solution.py:136
  297.6 1.8 convert_element_type.84
  (61 shorter events, 14.1 us)
Async XLA Ops:
  6.5 21.5 %copy-start = (bf16[512,1024]{1,0:T(8,128)(2,1)S(1)}, bf16[512,1024]{1,0:T(8,128)(2,1)}, u32[]{:S(2)}) copy-start(bf16[512,1024]{1,0:T(8,128)(2,1)} %param.23) | copy-start | bytes 3145732
  6.5 82.2 %all-gather.3.cloned.1.call-start = ((), (), s32[]{:S(2)}) async-start(), calls=%async_computation.4 | async-start | bytes 2654208 | tf_op jit(solution)/shard_map/all_gather | solution.py:93
  8.2 23.2 %collective-permute-start.1 = (bf16[256,512]{1,0:T(8,128)(2,1)S(1)}, bf16[256,512]{1,0:T(8,128)(2,1)}, u32[]{:S(2)}, u32[]{:S(2)}) collective-permute-start(bf16[256,512]{1,0:T(8,128)(2,1)S(1)} %slice.7), channel_id=1, source_target_pairs={{0,1},{1,2},{2,3},{3,4},{4,5},{5,6},{6,7},{8,9},{9,10},{10,11},{11... | collective-permute-start | bytes 786440 | tf_op jit(solution)/shard_map/ppermute | solution.py:15
  15.5 29.1 %collective-permute-start = (bf16[256,512]{1,0:T(8,128)(2,1)}, bf16[256,512]{1,0:T(8,128)(2,1)}, u32[]{:S(2)}, u32[]{:S(2)}) collective-permute-start(bf16[256,512]{1,0:T(8,128)(2,1)} %slice.6), channel_id=1, source_target_pairs={{0,1},{1,2},{2,3},{3,4},{4,5},{5,6},{6,7},{8,9},{9,10},{10,11},{11... | collective-permute-start | bytes 786440 | tf_op jit(solution)/shard_map/ppermute | solution.py:15
  22.0 30.8 %all-to-all-start = ((s32[4,2,1]{1,2,0:T(1,128)}), s32[4,2,1]{1,2,0:T(1,128)S(1)}, u32[]{:S(2)}, u32[]{:S(2)}) async-start(s32[4,2,1]{1,2,0:T(1,128)} %bitcast.11), calls=%async_computation | async-start | bytes 4096 | tf_op jit(solution)/shard_map/all_to_all | solution.py:90
  25.2 94.9 %all-gather.5.cloned.1.call-start = ((), (), s32[]{:S(2)}) async-start(), calls=%async_computation.5 | async-start | bytes 2654208 | tf_op jit(solution)/shard_map/all_gather | solution.py:94
  28.7 2.7 copy-start.1
  33.6 11.0 %copy-start.2 = (bf16[512,512]{1,0:T(8,128)(2,1)S(1)}, bf16[512,512]{1,0:T(8,128)(2,1)}, u32[]{:S(2)}) copy-start(bf16[512,512]{1,0:T(8,128)(2,1)} %param.16) | copy-start | bytes 1572868
  45.9 6.0 %copy-start.4 = (bf16[512,1024]{1,0:T(8,128)(2,1)S(1)}, bf16[512,1024]{1,0:T(8,128)(2,1)}, u32[]{:S(2)}) copy-start(bf16[512,1024]{1,0:T(8,128)(2,1)} %param.18) | copy-start | bytes 3145732
  45.9 6.0 %copy-start.5 = (bf16[512,1024]{1,0:T(8,128)(2,1)S(1)}, bf16[512,1024]{1,0:T(8,128)(2,1)}, u32[]{:S(2)}) copy-start(bf16[512,1024]{1,0:T(8,128)(2,1)} %param.17) | copy-start | bytes 3145732
  52.8 18.0 %all-to-all-start.2 = ((bf16[8,64,1024]{2,1,0:T(8,128)(2,1)}), bf16[8,64,1024]{2,1,0:T(8,128)(2,1)S(1)}, u32[]{:S(2)}, u32[]{:S(2)}) async-start(bf16[8,64,1024]{2,1,0:T(8,128)(2,1)} %copy.55), calls=%async_computation.2 | async-start | bytes 2097152 | tf_op jit(solution)/shard_map/all_to_all | solution.py:89
  57.9 62.1 %copy-start.3 = (bf16[3,384]{1,0:T(4,128)(2,1)S(1)}, bf16[3,384]{1,0:T(4,128)(2,1)}, u32[]{:S(2)}) copy-start(bf16[3,384]{1,0:T(4,128)(2,1)} %param.22) | copy-start | bytes 6916
  70.8 17.9 %all-to-all-start.1 = ((bf16[8,64,1024]{2,1,0:T(8,128)(2,1)}), bf16[8,64,1024]{2,1,0:T(8,128)(2,1)S(1)}, u32[]{:S(2)}, u32[]{:S(2)}) async-start(bf16[8,64,1024]{2,1,0:T(8,128)(2,1)} %copy.53), calls=%async_computation.1 | async-start | bytes 2097152 | tf_op jit(solution)/shard_map/all_to_all | solution.py:88
  74.3 223.3 %reduce-scatter.2.cloned.1.call-start = ((), (), s32[]{:S(2)}) async-start(), calls=%async_computation.6 | async-start | bytes 2654208 | tf_op jit(solution)/shard_map/reduce_scatter | solution.py:136
Sparse Core Ops, SparseCore 0:
  9.5 56.6 all-gather.2
  68.2 51.7 all-gather.4
  229.9 67.6 reduce-scatter.1
where the time goes:
time: 308 us; the launch traced here: 306 us
  waiting for transfers between devices  125 us (41%)
  matrix products  66 us (21%)
  loops' own time  35.5 us (12%)
  local copies, waits for them, and re-layouts  33.6 us (11%)
  starting transfers between devices  19.6 us (6%)
  between operations  13.3 us (4%)
  other arithmetic  13.1 us (4%)
    reduce_scatter x1, waiting for transfers between devices, body(): lax.psum_scatter((lax.fori_loop(0, slot_count, add_slot, start_acc) * inv...  67.9 us
    all_gather x1, waiting for transfers between devices, body(): lax.all_gather(w_up, 'seq', axis=2, tiled=True)  31.4 us
    dot_general x8, matrix products, add_slot(): lax.dot_general(columns, grad_all[slot_idx], (((0,), (0,)), ((), ())), pr...  23.6 us
    another operation x1, loops' own time, body(): lax.map(slot_terms, (got_rows, got_cot, safe_lang, live_slot))  22.4 us
    dynamic_slice x16, local copies, waits for them, and re-layouts, body(): lax.map(slot_terms, (got_rows, got_cot, safe_lang, live_slot))  16.1 us
    another operation x1, loops' own time, body(): lax.fori_loop(0, slot_count, add_slot, start_acc) * inv_scale  13.2 us
    all_to_all x1, waiting for transfers between devices, body(): lax.all_to_all(row_slots, 'grp', split_axis=0, concat_axis=0, tiled=True)  12.8 us
    dot_general x8, matrix products, slot_terms(): lax.dot_general(slot_cot, up_one, (((1,), (1,)), ((), ())), preferred_ele...  12.1 us
  transfers between devices with their start and end apart: 8, of which 4 were waited for; matrix products, arithmetic and copies ran while one was open for 12% of the time, Pallas kernels for 0%

commit v1 on v0

--- a/solution.py
+++ b/solution.py
@@ -7,6 +7,11 @@
 HD = 64
 WINDOW = 256
 EPSILON = 1e-05
+
+
+def remake_bars_all(point, peer_axis):
+    lower = lax.all_gather(point, peer_axis)
+    return jnp.concatenate(lower, axis=2)
 
 
 def shifted(value, axis, by):
@@ -91,7 +96,7 @@
     )
     down_all, up_all = (
         lax.all_gather(w_down, "seq", axis=1, tiled=True),
-        lax.all_gather(w_up, "seq", axis=2, tiled=True),
+        remake_bars_all(w_up, "seq"),
     )
     live_slot = got_lang >= 0
     safe_lang = jnp.where(live_slot, got_lang - lax.axis_index("grp") * lang_grp, 0).astype(

time: 308 us -> 296 us (0.961)
  loops' own time: 35.5 us -> 31.3 us
  waiting for transfers between devices: 125 us -> 121 us
  local copies, waits for them, and re-layouts: 33.6 us -> 30.1 us
    all_gather x1, waiting for transfers between devices: 31.4 us -> 0.01 us  [remake_bars_all(): lower = lax.all_gather(point, peer_axis)]
    all_gather x1, waiting for transfers between devices: 0.01 us -> 30.1 us  [body(): lax.all_gather(w_down, 'seq', axis=1, tiled=True)]
    dynamic_slice x16, local copies, waits for them, and re-layouts: 16.1 us -> 9.3 us  [body(): lax.map(slot_terms, (got_rows, got_cot, safe_lang, live_slot))]
    another operation x1, loops' own time: 22.4 us -> 18.2 us  [body(): lax.map(slot_terms, (got_rows, got_cot, safe_lang, live_slot))]
    reshape x0 -> x1, local copies, waits for them, and re-layouts: none -> 3.85 us  [remake_bars_all(): return jnp.concatenate(lower, axis=2)]
  transfers between devices with their start and end apart: 8 -> 8, of which waited for: 4 -> 4; matrix products, arithmetic and copies ran while one was open for 12% -> 13% of each run, Pallas kernels for 0% -> 0%
where the time goes in v1:
time: 296 us; the launch traced here: 294 us
  waiting for transfers between devices  121 us (41%)
  matrix products  66 us (22%)
  loops' own time  31.3 us (11%)
  local copies, waits for them, and re-layouts  30.1 us (10%)
  starting transfers between devices  19.6 us (7%)
  between operations  13.3 us (4%)
  other arithmetic  12.5 us (4%)
    reduce_scatter x1, waiting for transfers between devices, body(): lax.psum_scatter((lax.fori_loop(0, slot_count, add_slot, start_acc) * inv...  68.3 us
    all_gather x1, waiting for transfers between devices, body(): lax.all_gather(w_down, 'seq', axis=1, tiled=True)  30.1 us
    dot_general x8, matrix products, add_slot(): lax.dot_general(columns, grad_all[slot_idx], (((0,), (0,)), ((), ())), pr...  23.6 us
    another operation x1, loops' own time, body(): lax.map(slot_terms, (got_rows, got_cot, safe_lang, live_slot))  18.2 us
    another operation x1, loops' own time, body(): lax.fori_loop(0, slot_count, add_slot, start_acc) * inv_scale  13.2 us
    dot_general x8, matrix products, slot_terms(): lax.dot_general(slot_cot, up_one, (((1,), (1,)), ((), ())), preferred_ele...  12.1 us
    all_to_all x1, waiting for transfers between devices, body(): lax.all_to_all(cot_slots, 'grp', split_axis=0, concat_axis=0, tiled=True)  11.3 us
    dot_general x8, matrix products, slot_terms(): jnp.dot(slot_rows, down_one, preferred_element_type=jnp.float32) + bias_one  11.1 us
  transfers between devices with their start and end apart: 8, of which 4 were waited for; matrix products, arithmetic and copies ran while one was open for 13% of the time, Pallas kernels for 0%

profile of v1, /device:TPU:0, one launch (start us, length us, event | category | flops | bytes accessed | tf_op | source)
XLA Modules:
  0.0 294.1 jit_solution(3364677107052313102)
XLA Ops:
  6.5 0.7 all-gather.6.cloned.1.call-update
  7.3 1.0 slice.7
  8.2 5.6 %collective-permute-start.1 = (bf16[256,512]{1,0:T(8,128)(2,1)S(1)}, bf16[256,512]{1,0:T(8,128)(2,1)}, u32[]{:S(2)}, u32[]{:S(2)}) collective-permute-start(bf16[256,512]{1,0:T(8,128)(2,1)S(1)} %slice.7), channel_id=1, source_target_pairs={{0,1},{1,2},{2,3},{3,4},{4,5},{5,6},{6,7},{8,9},{9,10},{10,11},{11... | collective-permute-start | bytes 786440 | tf_op jit(solution)/shard_map/ppermute | solution.py:20
  13.8 1.7 slice.6
  15.5 3.5 %collective-permute-start = (bf16[256,512]{1,0:T(8,128)(2,1)}, bf16[256,512]{1,0:T(8,128)(2,1)}, u32[]{:S(2)}, u32[]{:S(2)}) collective-permute-start(bf16[256,512]{1,0:T(8,128)(2,1)} %slice.6), channel_id=1, source_target_pairs={{0,1},{1,2},{2,3},{3,4},{4,5},{5,6},{6,7},{8,9},{9,10},{10,11},{11... | collective-permute-start | bytes 786440 | tf_op jit(solution)/shard_map/ppermute | solution.py:20
  19.0 0.7 and_select_fusion
  19.8 0.7 multiply_add_fusion
  20.5 0.8 convert_reduce_fusion.2
  21.3 0.7 sub.43
  22.0 3.2 %all-to-all-start = ((s32[4,2,1]{1,2,0:T(1,128)}), s32[4,2,1]{1,2,0:T(1,128)S(1)}, u32[]{:S(2)}, u32[]{:S(2)}) async-start(s32[4,2,1]{1,2,0:T(1,128)} %bitcast.11), calls=%async_computation | async-start | bytes 4096 | tf_op jit(solution)/shard_map/all_to_all | solution.py:95
  25.2 0.7 all-gather.4.cloned.1.call-update
  25.9 2.1 copy.54
  28.0 0.7 convolution_convert_fusion
  28.7 1.6 copy.59
  30.3 1.1 fusion.39
  31.4 1.0 pad_maximum_fusion.1
  32.4 1.2 copy.53
  33.6 11.0 %fusion.53 = (f32[8,512]{1,0:T(8,128)S(1)}, f32[8,512,768]{1,2,0:T(8,128)}) fusion(f32[512,768]{0,1:T(8,128)S(1)} %get-tuple-element.273, bf16[768,8,64]{0,2,1:T(8,128)(2,1)} %bitcast.93, bf16[512,8,64]{0,2,1:T(8,128)(2,1)} %bitcast.95, pred[512,768]{0,1:T(8,128)(4,1)} %get-tuple-element.272), kind=kOutput, calls=%fused_computation.86 | convolution fusion | flops 418382592 | bytes 15876096 | tf_op jit(solution)/shard_map/sub | solution.py:57
  44.6 1.0 pad_maximum_fusion
  45.9 6.0 %fusion.40 = bf16[8,64,512]{2,1,0:T(8,128)(2,1)S(1)} fusion(bf16[768,8,64]{0,2,1:T(8,128)(2,1)S(1)} %bitcast.94, f32[8,512,768]{1,2,0:T(8,128)} %get-tuple-element.275, f32[8,512]{1,0:T(8,128)S(1)} %get-tuple-element.274), kind=kOutput, calls=%fused_computation.57 | convolution fusion | flops 409206784 | bytes 13910016 | tf_op jit(solution)/shard_map/hqk,khd->qhd/dot_general | solution.py:59
  51.9 0.8 convert_reduce_fusion.1
  52.8 3.7 %all-to-all-start.2 = ((bf16[8,64,1024]{2,1,0:T(8,128)(2,1)}), bf16[8,64,1024]{2,1,0:T(8,128)(2,1)S(1)}, u32[]{:S(2)}, u32[]{:S(2)}) async-start(bf16[8,64,1024]{2,1,0:T(8,128)(2,1)} %copy.59), calls=%async_computation.2 | async-start | bytes 2097152 | tf_op jit(solution)/shard_map/all_to_all | solution.py:94
  57.2 0.7 convolution_convert_fusion.1
  57.9 1.6 copy.57
  59.5 11.3 %all-to-all-done.2 = bf16[8,64,1024]{2,1,0:T(8,128)(2,1)S(1)} async-done(((bf16[8,64,1024]{2,1,0:T(8,128)(2,1)}), bf16[8,64,1024]{2,1,0:T(8,128)(2,1)S(1)}, u32[]{:S(2)}, u32[]{:S(2)}) %all-to-all-start.2) | async-done | bytes 1048608 | tf_op jit(solution)/shard_map/all_to_all | solution.py:94
  70.8 3.5 %all-to-all-start.1 = ((bf16[8,64,1024]{2,1,0:T(8,128)(2,1)}), bf16[8,64,1024]{2,1,0:T(8,128)(2,1)S(1)}, u32[]{:S(2)}, u32[]{:S(2)}) async-start(bf16[8,64,1024]{2,1,0:T(8,128)(2,1)} %copy.57), calls=%async_computation.1 | async-start | bytes 2097152 | tf_op jit(solution)/shard_map/all_to_all | solution.py:93
  74.6 3.8 %copy.68 = bf16[8,3,48,8,128]{4,3,0,2,1:T(8,128)(2,1)} copy(bf16[8,3,48,8,128]{4,3,2,1,0:T(8,128)(2,1)} %bitcast.91) | data formatting | bytes 4718592 | tf_op jit(solution)/shard_map/reshape | solution.py:14
  78.5 10.2 %all-to-all-done.1 = bf16[8,64,1024]{2,1,0:T(8,128)(2,1)S(1)} async-done(((bf16[8,64,1024]{2,1,0:T(8,128)(2,1)}), bf16[8,64,1024]{2,1,0:T(8,128)(2,1)S(1)}, u32[]{:S(2)}, u32[]{:S(2)}) %all-to-all-start.1) | async-done | bytes 1048608 | tf_op jit(solution)/shard_map/all_to_all | solution.py:93
  88.7 30.1 %all-gather.4.cloned.1.call-done = bf16[3,1024,384]{2,1,0:T(8,128)(2,1)} async-done(((bf16[3,128,384]{2,1,0:T(8,128)(2,1)}), bf16[3,1024,384]{2,1,0:T(8,128)(2,1)}) %all-gather.4.cloned.1.call-update) | async-done | bytes 2359312 | tf_op jit(solution)/shard_map/all_gather | solution.py:98
  118.8 50.8 %while.25 = (s32[]{:T(128)}, bf16[8,64,384]{2,1,0:T(8,128)(2,1)S(1)}, bf16[8,64,1024]{2,1,0:T(8,128)(2,1)S(1)}, s32[8]{0:T(128)S(1)}, bf16[3,1024,384]{2,1,0:T(8...) while((s32[]{:T(128)}, ...), condition=%wide.region_8.9_spmd, body=%wide.region_7.8_spmd.sunk | while | flops 101179776 | bytes 2087354 | solution.py:122
  121.1 1.4 convolution_add_fusion.2
  122.5 0.6 dynamic_slice.120
  123.6 1.5 fusion.73
  127.4 1.4 convolution_add_fusion.2
  128.8 0.6 dynamic_slice.120
  130.0 1.5 fusion.73
  133.8 1.4 convolution_add_fusion.2
  135.2 0.6 dynamic_slice.120
  136.3 1.5 fusion.73
  140.1 1.4 convolution_add_fusion.2
  141.5 0.6 dynamic_slice.120
  142.7 1.5 fusion.73
  146.5 1.4 convolution_add_fusion.2
  149.0 1.5 fusion.73
  152.8 1.4 convolution_add_fusion.2
  155.4 1.5 fusion.73
  159.2 1.4 convolution_add_fusion.2
  161.7 1.5 fusion.73
  165.5 1.4 convolution_add_fusion.2
  166.9 0.6 dynamic_slice.120
  168.1 1.5 fusion.73
  169.6 2.4 broadcast_in_dim.50
  172.0 41.2 %while.26 = (s32[]{:T(128)}, f32[1024,3,384]{2,0,1:T(8,128)}, s32[8]{0:T(128)S(1)}, bf16[8,64,1024]{2,1,0:T(8,128)(2,1)S(1)}, bf16[8,64,384]{2,1,0:T(8,128)(2,1)S(1)}, /*index=5*/s32[]{:T(128)}, s32[]{:T(128)}, s32[]{:T(128)}) while((s32[]{:T(128)}, f32[1024,3,384]{2,0,1:T(8,128)}, s32[8]{0:T(128)S(1)}, bf16[8,64,1024]{2,1,0:T(8,128)(2,1)S(1)}, ...), condition=%wide.region_10.11_spmd, body=%wide.region_9.10_spmd.sunk | while | flops 50724868 | bytes 3327111 | solution.py:142
  174.2 3.0 %fusion.76 = f32[1024,3,384]{2,0,1:T(8,128)} fusion(f32[1024,3,384]{2,0,1:T(8,128)} %get-tuple-element.409, s32[]{:T(128)S(6)} %select_n.61, bf16[8,64,1024]{2,1,0:T(8,128)(2,1)S(1)} %get-tuple-element.419, s32[]{:T(128)} %get-tuple-element.408, bf16[8,64,384]{2,1,0:T(8,128)(2,1)S(1)} %get-tuple-element.420), kind=kOutput, calls=%fused_computation.1.clone.1 | convolution fusion | flops 50724864 | bytes 3326980 | tf_op jit(solution)/shard_map/while/body/eval_jaxpr/dot_general | solution.py:127
  179.4 3.0 %fusion.76 = f32[1024,3,384]{2,0,1:T(8,128)} fusion(f32[1024,3,384]{2,0,1:T(8,128)} %get-tuple-element.409, s32[]{:T(128)S(6)} %select_n.61, bf16[8,64,1024]{2,1,0:T(8,128)(2,1)S(1)} %get-tuple-element.419, s32[]{:T(128)} %get-tuple-element.408, bf16[8,64,384]{2,1,0:T(8,128)(2,1)S(1)} %get-tuple-element.420), kind=kOutput, calls=%fused_computation.1.clone.1 | convolution fusion | flops 50724864 | bytes 3326980 | tf_op jit(solution)/shard_map/while/body/eval_jaxpr/dot_general | solution.py:127
  184.5 2.9 %fusion.76 = f32[1024,3,384]{2,0,1:T(8,128)} fusion(f32[1024,3,384]{2,0,1:T(8,128)} %get-tuple-element.409, s32[]{:T(128)S(6)} %select_n.61, bf16[8,64,1024]{2,1,0:T(8,128)(2,1)S(1)} %get-tuple-element.419, s32[]{:T(128)} %get-tuple-element.408, bf16[8,64,384]{2,1,0:T(8,128)(2,1)S(1)} %get-tuple-element.420), kind=kOutput, calls=%fused_computation.1.clone.1 | convolution fusion | flops 50724864 | bytes 3326980 | tf_op jit(solution)/shard_map/while/body/eval_jaxpr/dot_general | solution.py:127
  189.7 2.9 %fusion.76 = f32[1024,3,384]{2,0,1:T(8,128)} fusion(f32[1024,3,384]{2,0,1:T(8,128)} %get-tuple-element.409, s32[]{:T(128)S(6)} %select_n.61, bf16[8,64,1024]{2,1,0:T(8,128)(2,1)S(1)} %get-tuple-element.419, s32[]{:T(128)} %get-tuple-element.408, bf16[8,64,384]{2,1,0:T(8,128)(2,1)S(1)} %get-tuple-element.420), kind=kOutput, calls=%fused_computation.1.clone.1 | convolution fusion | flops 50724864 | bytes 3326980 | tf_op jit(solution)/shard_map/while/body/eval_jaxpr/dot_general | solution.py:127
  194.8 2.9 %fusion.76 = f32[1024,3,384]{2,0,1:T(8,128)} fusion(f32[1024,3,384]{2,0,1:T(8,128)} %get-tuple-element.409, s32[]{:T(128)S(6)} %select_n.61, bf16[8,64,1024]{2,1,0:T(8,128)(2,1)S(1)} %get-tuple-element.419, s32[]{:T(128)} %get-tuple-element.408, bf16[8,64,384]{2,1,0:T(8,128)(2,1)S(1)} %get-tuple-element.420), kind=kOutput, calls=%fused_computation.1.clone.1 | convolution fusion | flops 50724864 | bytes 3326980 | tf_op jit(solution)/shard_map/while/body/eval_jaxpr/dot_general | solution.py:127
  200.0 2.9 %fusion.76 = f32[1024,3,384]{2,0,1:T(8,128)} fusion(f32[1024,3,384]{2,0,1:T(8,128)} %get-tuple-element.409, s32[]{:T(128)S(6)} %select_n.61, bf16[8,64,1024]{2,1,0:T(8,128)(2,1)S(1)} %get-tuple-element.419, s32[]{:T(128)} %get-tuple-element.408, bf16[8,64,384]{2,1,0:T(8,128)(2,1)S(1)} %get-tuple-element.420), kind=kOutput, calls=%fused_computation.1.clone.1 | convolution fusion | flops 50724864 | bytes 3326980 | tf_op jit(solution)/shard_map/while/body/eval_jaxpr/dot_general | solution.py:127
  205.1 3.0 %fusion.76 = f32[1024,3,384]{2,0,1:T(8,128)} fusion(f32[1024,3,384]{2,0,1:T(8,128)} %get-tuple-element.409, s32[]{:T(128)S(6)} %select_n.61, bf16[8,64,1024]{2,1,0:T(8,128)(2,1)S(1)} %get-tuple-element.419, s32[]{:T(128)} %get-tuple-element.408, bf16[8,64,384]{2,1,0:T(8,128)(2,1)S(1)} %get-tuple-element.420), kind=kOutput, calls=%fused_computation.1.clone.1 | convolution fusion | flops 50724864 | bytes 3326980 | tf_op jit(solution)/shard_map/while/body/eval_jaxpr/dot_general | solution.py:127
  210.3 2.9 %fusion.76 = f32[1024,3,384]{2,0,1:T(8,128)} fusion(f32[1024,3,384]{2,0,1:T(8,128)} %get-tuple-element.409, s32[]{:T(128)S(6)} %select_n.61, bf16[8,64,1024]{2,1,0:T(8,128)(2,1)S(1)} %get-tuple-element.419, s32[]{:T(128)} %get-tuple-element.408, bf16[8,64,384]{2,1,0:T(8,128)(2,1)S(1)} %get-tuple-element.420), kind=kOutput, calls=%fused_computation.1.clone.1 | convolution fusion | flops 50724864 | bytes 3326980 | tf_op jit(solution)/shard_map/while/body/eval_jaxpr/dot_general | solution.py:127
  213.2 4.2 %multiply_convert_fusion = bf16[1024,3,384]{2,0,1:T(8,128)(2,1)} fusion(f32[1024,3,384]{2,0,1:T(8,128)} %get-tuple-element.213), kind=kLoop, calls=%fused_computation.42 | loop fusion | flops 2359296 | bytes 7077888 | tf_op jit(solution)/shard_map/convert_element_type | solution.py:142
  217.4 68.3 %reduce-scatter.2.cloned.1.call-done = bf16[128,3,384]{2,0,1:T(8,128)(2,1)} async-done(((bf16[1024,3,384]{2,0,1:T(8,128)(2,1)}), bf16[128,3,384]{2,0,1:T(8,128)(2,1)}) %reduce-scatter.2.cloned.1.call-update) | async-done | bytes 294928 | tf_op jit(solution)/shard_map/reduce_scatter | solution.py:141
  285.7 1.8 convert_element_type.84
  (62 shorter events, 12.6 us)
Async XLA Ops:
  6.5 21.5 %copy-start = (bf16[512,1024]{1,0:T(8,128)(2,1)S(1)}, bf16[512,1024]{1,0:T(8,128)(2,1)}, u32[]{:S(2)}) copy-start(bf16[512,1024]{1,0:T(8,128)(2,1)} %param.23) | copy-start | bytes 3145732
  6.5 68.1 %all-gather.6.cloned.1.call-start = ((), (), s32[]{:S(2)}) async-start(), calls=%async_computation.6 | async-start | bytes 2654208 | tf_op jit(solution)/shard_map/all_gather | solution.py:13
  8.2 23.2 %collective-permute-start.1 = (bf16[256,512]{1,0:T(8,128)(2,1)S(1)}, bf16[256,512]{1,0:T(8,128)(2,1)}, u32[]{:S(2)}, u32[]{:S(2)}) collective-permute-start(bf16[256,512]{1,0:T(8,128)(2,1)S(1)} %slice.7), channel_id=1, source_target_pairs={{0,1},{1,2},{2,3},{3,4},{4,5},{5,6},{6,7},{8,9},{9,10},{10,11},{11... | collective-permute-start | bytes 786440 | tf_op jit(solution)/shard_map/ppermute | solution.py:20
  15.5 29.1 %collective-permute-start = (bf16[256,512]{1,0:T(8,128)(2,1)}, bf16[256,512]{1,0:T(8,128)(2,1)}, u32[]{:S(2)}, u32[]{:S(2)}) collective-permute-start(bf16[256,512]{1,0:T(8,128)(2,1)} %slice.6), channel_id=1, source_target_pairs={{0,1},{1,2},{2,3},{3,4},{4,5},{5,6},{6,7},{8,9},{9,10},{10,11},{11... | collective-permute-start | bytes 786440 | tf_op jit(solution)/shard_map/ppermute | solution.py:20
  22.0 30.8 %all-to-all-start = ((s32[4,2,1]{1,2,0:T(1,128)}), s32[4,2,1]{1,2,0:T(1,128)S(1)}, u32[]{:S(2)}, u32[]{:S(2)}) async-start(s32[4,2,1]{1,2,0:T(1,128)} %bitcast.11), calls=%async_computation | async-start | bytes 4096 | tf_op jit(solution)/shard_map/all_to_all | solution.py:95
  25.2 93.6 %all-gather.4.cloned.1.call-start = ((), (), s32[]{:S(2)}) async-start(), calls=%async_computation.4 | async-start | bytes 2654208 | tf_op jit(solution)/shard_map/all_gather | solution.py:98
  28.7 2.7 copy-start.1
  33.6 11.0 %copy-start.2 = (bf16[512,512]{1,0:T(8,128)(2,1)S(1)}, bf16[512,512]{1,0:T(8,128)(2,1)}, u32[]{:S(2)}) copy-start(bf16[512,512]{1,0:T(8,128)(2,1)} %param.16) | copy-start | bytes 1572868
  45.9 6.0 %copy-start.4 = (bf16[512,1024]{1,0:T(8,128)(2,1)S(1)}, bf16[512,1024]{1,0:T(8,128)(2,1)}, u32[]{:S(2)}) copy-start(bf16[512,1024]{1,0:T(8,128)(2,1)} %param.18) | copy-start | bytes 3145732
  45.9 6.0 %copy-start.5 = (bf16[512,1024]{1,0:T(8,128)(2,1)S(1)}, bf16[512,1024]{1,0:T(8,128)(2,1)}, u32[]{:S(2)}) copy-start(bf16[512,1024]{1,0:T(8,128)(2,1)} %param.17) | copy-start | bytes 3145732
  52.8 18.0 %all-to-all-start.2 = ((bf16[8,64,1024]{2,1,0:T(8,128)(2,1)}), bf16[8,64,1024]{2,1,0:T(8,128)(2,1)S(1)}, u32[]{:S(2)}, u32[]{:S(2)}) async-start(bf16[8,64,1024]{2,1,0:T(8,128)(2,1)} %copy.59), calls=%async_computation.2 | async-start | bytes 2097152 | tf_op jit(solution)/shard_map/all_to_all | solution.py:94
  70.8 17.9 %all-to-all-start.1 = ((bf16[8,64,1024]{2,1,0:T(8,128)(2,1)}), bf16[8,64,1024]{2,1,0:T(8,128)(2,1)S(1)}, u32[]{:S(2)}, u32[]{:S(2)}) async-start(bf16[8,64,1024]{2,1,0:T(8,128)(2,1)} %copy.57), calls=%async_computation.1 | async-start | bytes 2097152 | tf_op jit(solution)/shard_map/all_to_all | solution.py:93
  74.3 211.4 %reduce-scatter.2.cloned.1.call-start = ((), (), s32[]{:S(2)}) async-start(), calls=%async_computation.5 | async-start | bytes 2654208 | tf_op jit(solution)/shard_map/reduce_scatter | solution.py:141
  74.6 44.1 %copy-start.3 = (bf16[3,384]{1,0:T(4,128)(2,1)S(1)}, bf16[3,384]{1,0:T(4,128)(2,1)}, u32[]{:S(2)}) copy-start(bf16[3,384]{1,0:T(4,128)(2,1)} %param.22) | copy-start | bytes 6916
Sparse Core Ops, SparseCore 0:
  9.5 56.6 all-gather.5
  68.4 50.3 all-gather.3
  217.6 68.1 reduce-scatter.1
